TPU v7x, 32 devices: a whole 2x2x4 slice. The times are simulated.
32 devices in a mesh: grp: 2 (over y), row: 4 (over z), col: 4 (over x, core).
Axes of the slice: x: 2, y: 2, z: 4, core: 2. Of those that a mesh axis runs over, the one named last changes fastest.
Arguments:
- activations: bfloat16 [1024, 6144], P(('grp', 'col'), 'row'), parts along dimension 0, may hold values from -6 to 6
- out_grads: bfloat16 [1024, 18432], P(('grp', 'row'), 'col'), parts along dimension 0, may hold values from -0.1796875 to 0.1796875
- matrix: bfloat16 [12288, 18432], P(('grp', 'row'), 'col'), parts along dimension 0, may hold values from -30 to 30
- left: bfloat16 [12288, 256], P(('grp', 'row')), parts along dimension 0, may hold values from -4 to 4
- right: bfloat16 [36864, 256], P(('grp', 'col')), parts along dimension 0, may hold values from -4 to 4
Outputs:
- left_new: bfloat16 [12288, 256], P(('grp', 'row')), parts along dimension 0
- right_new: bfloat16 [36864, 256], P(('grp', 'col')), parts along dimension 0
- residual: bfloat16 [12288, 18432], P(('grp', 'row'), 'col'), parts along dimension 0
There are 2 independent parts, one for each index of `grp`. A program takes and returns all parts, laid end to end along the dimension named above; each array names one. Nothing has to cross between parts.
All inputs are finite; a program needn't handle non-finite values.
Results may differ from a plain program's by a relative error of at most 0.0034.
Values may be sent and summed in bfloat16 or wider, within the bound.
A program may use at most 192 MiB of HBM per device.

v0:
```python
import jax
import jax.numpy as jnp
from jax import lax
from jax.sharding import PartitionSpec as P

epsilon = 1e-06


def contract_rank(first, second):
    return lax.dot_general(
        first, second, (((1,), (1,)), ((), ())), preferred_element_type=jnp.float32
    )


def contract_tokens(first, second):
    return lax.dot_general(
        first, second, (((0,), (0,)), ((), ())), preferred_element_type=jnp.float32
    )


def body(activations, out_grads, matrix, left, right):
    col_count = lax.axis_size("col")
    row_count = lax.axis_size("row")
    gathered = lax.all_gather(activations, "col", axis=0, tiled=True)
    grads_full = lax.all_gather(out_grads, "row", axis=0, tiled=True)
    gradient = contract_tokens(gathered, grads_full)
    wfloat = matrix.astype(jnp.float32)
    fisher = 1.0 + (wfloat * gradient) ** 2
    early_residual = wfloat - contract_rank(left, right)
    weighted_early = (fisher * early_residual).astype(jnp.bfloat16)
    left_partial = jnp.dot(weighted_early, right, preferred_element_type=jnp.float32)
    left_descent = lax.psum(left_partial, "col")
    left_round = left_descent.astype(jnp.bfloat16)
    left_norm_term = jnp.sum(left_descent * left_descent) / col_count
    left_image = contract_rank(left_round, right)
    left_curve, left_norm = lax.psum(
        (jnp.sum(fisher * left_image * left_image), left_norm_term), ("row", "col")
    )
    left_step = left_norm / (left_curve + epsilon)
    left_new = (left.astype(jnp.float32) + left_step * left_descent).astype(jnp.bfloat16)
    later_residual = early_residual - left_step * left_image
    weighted_later = (fisher * later_residual).astype(jnp.bfloat16)
    right_partial = contract_tokens(weighted_later, left_new)
    right_descent = lax.psum(right_partial.astype(jnp.bfloat16), "row").astype(jnp.float32)
    right_round = right_descent.astype(jnp.bfloat16)
    right_norm_term = jnp.sum(right_descent * right_descent) / row_count
    right_image = contract_rank(left_new, right_round)
    right_curve, right_norm = lax.psum(
        (jnp.sum(fisher * right_image * right_image), right_norm_term), ("row", "col")
    )
    right_step = right_norm / (right_curve + epsilon)
    right_new = (right.astype(jnp.float32) + right_step * right_descent).astype(jnp.bfloat16)
    residual = (later_residual - right_step * right_image).astype(jnp.bfloat16)
    return (left_new, right_new, residual)


def solution(mesh):
    placed = (
        P(("grp", "col"), "row"),
        P(("grp", "row"), "col"),
        P(("grp", "row"), "col"),
        P(("grp", "row"), None),
        P(("grp", "col"), None),
    )
    return jax.shard_map(
        body,
        mesh=mesh,
        in_specs=placed,
        out_specs=(P(("grp", "row"), None), P(("grp", "col"), None), P(("grp", "row"), "col")),
        check_vma=False,
    )
```

profile of v0, /device:TPU:0, one launch (start us, length us, event | category | flops | bytes accessed | tf_op | source)
XLA Modules:
  0.0 489.8 jit_solution(9094421947014775079)
XLA Ops:
  7.2 0.0 all-gather.3.cloned.1.call-start
  7.2 0.7 all-gather.3.cloned.1.call-update
  7.9 0.0 all-gather.5.cloned.1.call-start
  7.9 0.7 all-gather.5.cloned.1.call-update
  8.6 0.0 all-reduce.5.cloned.1.call-start
  8.7 19.6 %convert_subtract_fusion = f32[1536,4608]{1,0:T(8,128)} fusion(bf16[1536,4608]{1,0:T(8,128)(2,1)} %param.7, bf16[1536,256]{1,0:T(8,128)(2,1)} %param.8, bf16[4608,256]{1,0:T(8,128)(2,1)} %param.9), kind=kOutput, calls=%fused_computation.2 | convolution fusion | flops 3638034432 | bytes 45613056 | tf_op jit(solution)/shard_map/dot_general | solution.py:10
  28.3 0.0 copy-start
  28.3 3.6 all-gather.3.cloned.1.call-done
  31.9 91.0 %all-gather.5.cloned.1.call-done = bf16[512,4608]{1,0:T(8,128)(2,1)} async-done(((bf16[128,4608]{1,0:T(8,128)(2,1)}), bf16[512,4608]{1,0:T(8,128)(2,1)}) %all-gather.5.cloned.1.call-update) | async-done | bytes 4718608 | tf_op jit(solution)/shard_map/all_gather | solution.py:25
  122.9 17.9 %fusion.1 = f32[1536,4608]{1,0:T(8,128)} fusion(bf16[1536,4608]{1,0:T(8,128)(2,1)} %param.7, bf16[512,1536]{1,0:T(8,128)(2,1)} %all-gather.3.cloned.1.call-done, bf16[512,4608]{1,0:T(8,128)(2,1)} %all-gather.5.cloned.1.call-done), kind=kOutput, calls=%fused_computation.5 | convolution fusion | flops 7276068864 | bytes 48758784 | tf_op jit(solution)/shard_map/dot_general | solution.py:16
  140.8 0.0 copy-done
  140.8 19.9 %fusion.4 = f32[1536,256]{1,0:T(8,128)} fusion(bf16[4608,256]{1,0:T(8,128)(2,1)S(1)} %copy-done, f32[1536,4608]{1,0:T(8,128)} %fusion.1, f32[1536,4608]{1,0:T(8,128)} %convert_subtract_fusion), kind=kOutput, calls=%fused_computation.12 | convolution fusion | flops 3638034432 | bytes 60555264 | tf_op jit(solution)/shard_map/dot_general | solution.py:31
  160.7 0.0 all-reduce.5.cloned.1.call-update
  160.7 0.2 all-reduce.7.cloned.1.call-start
  160.9 41.2 %all-reduce.5.cloned.1.call-done = f32[1536,256]{1,0:T(8,128)} async-done(((f32[1536,256]{1,0:T(8,128)}), f32[1536,256]{1,0:T(8,128)}) %all-reduce.5.cloned.1.call-update) | async-done | bytes 1572880 | tf_op jit(solution)/shard_map/psum | solution.py:32
  202.1 2.4 multiply_reduce_fusion
  205.2 23.8 %fusion.2 = (f32[]{:T(128)}, f32[1536,4608]{1,0:T(8,128)}) fusion(f32[1536,4608]{1,0:T(8,128)} %fusion.1, bf16[4608,256]{1,0:T(8,128)(2,1)S(1)} %copy-done, f32[1536,256]{1,0:T(8,128)} %all-reduce.5.cloned.1.call-done), kind=kOutput, calls=%fused_computation.6 | convolution fusion | flops 3645505536 | bytes 60555268 | tf_op jit(solution)/shard_map/dot_general | solution.py:10
  229.0 32.8 %all-reduce.1 = (f32[]{:T(128)}, f32[]{:T(128)}) all-reduce(f32[]{:T(128)S(6)} %div.12, f32[]{:T(128)} %get-tuple-element.7), channel_id=1, replica_groups=mesh['grp'=2,'row'=4,'col'=4] {'row','col'}, use_global_device_ids=true, to_apply=%region_2.0 | all-reduce | flops 2 | bytes 16 | tf_op jit(solution)/shard_map/psum | solution.py:36
  263.1 1.8 add_convert_fusion
  264.9 0.0 copy-start.2
  264.9 30.2 %fusion.6 = bf16[4608,256]{1,0:T(8,128)(2,1)} fusion(bf16[1536,256]{1,0:T(8,128)(2,1)S(1)} %add_convert_fusion, f32[1536,4608]{1,0:T(8,128)} %fusion.1, f32[1536,4608]{1,0:T(8,128)} %convert_subtract_fusion, f32[1536,4608]{1,0:T(8,128)} %get-tuple-element.8, f32[]{:T(128)S(6)} %div.13), kind=kOutput, calls=%fused_computation.14 | convolution fusion | flops 3653369856 | bytes 88080384 | tf_op jit(solution)/shard_map/dot_general | solution.py:16
  295.1 0.0 all-reduce.7.cloned.1.call-update
  295.2 92.0 %all-reduce.7.cloned.1.call-done = bf16[4608,256]{1,0:T(8,128)(2,1)} async-done(((bf16[4608,256]{1,0:T(8,128)(2,1)}), bf16[4608,256]{1,0:T(8,128)(2,1)}) %all-reduce.7.cloned.1.call-update) | async-done | bytes 2359312 | tf_op jit(solution)/shard_map/psum | solution.py:44
  387.2 3.5 fusion.7
  391.3 0.0 copy-done.2
  391.3 23.9 %fusion.3 = (f32[]{:T(128)}, f32[1536,4608]{1,0:T(8,128)}) fusion(f32[1536,4608]{1,0:T(8,128)} %fusion.1, bf16[1536,256]{1,0:T(8,128)(2,1)S(1)} %add_convert_fusion, bf16[4608,256]{1,0:T(8,128)(2,1)} %all-reduce.7.cloned.1.call-done), kind=kOutput, calls=%fused_computation.7 | convolution fusion | flops 3645112320 | bytes 59768836 | tf_op jit(solution)/shard_map/dot_general | solution.py:10
  415.2 32.0 %all-reduce = (f32[]{:T(128)}, f32[]{:T(128)}) all-reduce(f32[]{:T(128)S(6)} %div.14, f32[]{:T(128)} %get-tuple-element.9), channel_id=1, replica_groups=mesh['grp'=2,'row'=4,'col'=4] {'row','col'}, use_global_device_ids=true, to_apply=%region_7.0 | all-reduce | flops 2 | bytes 16 | tf_op jit(solution)/shard_map/psum | solution.py:48
  448.5 0.0 copy-start.1
  448.5 32.5 %subtract_convert_fusion = bf16[1536,4608]{1,0:T(8,128)(2,1)} fusion(f32[1536,4608]{1,0:T(8,128)} %get-tuple-element.10, f32[]{:T(128)S(6)} %div.15, f32[1536,4608]{1,0:T(8,128)} %convert_subtract_fusion, f32[1536,4608]{1,0:T(8,128)} %get-tuple-element.8, f32[]{:T(128)S(6)} %div.13), kind=kLoop, calls=%fused_computation.8 | loop fusion | flops 35389440 | bytes 99090440 | tf_op jit(solution)/shard_map/convert_element_type | solution.py:53
  481.0 0.0 copy-done.1
  481.0 2.3 fusion.9
Async XLA Ops:
  7.2 24.8 %all-gather.3.cloned.1.call-start = ((), (), s32[]{:S(2)}) async-start(), calls=%async_computation | async-start | bytes 1966080 | tf_op jit(solution)/shard_map/all_gather | solution.py:24
  7.9 115.0 %all-gather.5.cloned.1.call-start = ((), (), s32[]{:S(2)}) async-start(), calls=%async_computation.1 | async-start | bytes 5898240 | tf_op jit(solution)/shard_map/all_gather | solution.py:25
  8.6 193.4 %all-reduce.5.cloned.1.call-start = ((), (), s32[]{:S(2)}) async-start(), calls=%async_computation.2 | async-start | bytes 3145728 | tf_op jit(solution)/shard_map/psum | solution.py:32
  28.3 112.5 %copy-start = (bf16[4608,256]{1,0:T(8,128)(2,1)S(1)}, bf16[4608,256]{1,0:T(8,128)(2,1)}, u32[]{:S(2)}) copy-start(bf16[4608,256]{1,0:T(8,128)(2,1)} %param.9) | copy-start | bytes 7077892
  160.7 226.5 %all-reduce.7.cloned.1.call-start = ((), (), s32[]{:S(2)}) async-start(), calls=%async_computation.3 | async-start | bytes 4718592 | tf_op jit(solution)/shard_map/psum | solution.py:44
  264.9 126.4 %copy-start.2 = (bf16[1536,256]{1,0:T(8,128)(2,1)}, bf16[1536,256]{1,0:T(8,128)(2,1)S(1)}, u32[]{:S(2)}) copy-start(bf16[1536,256]{1,0:T(8,128)(2,1)S(1)} %add_convert_fusion) | copy-start | bytes 2359300
  448.5 32.6 %copy-start.1 = (bf16[4608,256]{1,0:T(8,128)(2,1)S(1)}, bf16[4608,256]{1,0:T(8,128)(2,1)}, u32[]{:S(2)}) copy-start(bf16[4608,256]{1,0:T(8,128)(2,1)} %all-reduce.7.cloned.1.call-done) | copy-start | bytes 7077892
Sparse Core Ops, SparseCore 0:
  9.5 22.3 all-gather.2
  33.5 89.3 all-gather.4
  160.8 41.2 all-reduce.4
  295.3 91.8 all-reduce.6
where the time goes:
time: 490 us
  waiting for transfers between devices  229 us (47%)
  matrix products  135 us (28%)
  blocking collectives  64.8 us (13%)
  other arithmetic  42.5 us (9%)
  between operations  17.7 us (4%)
    psum x1, waiting for transfers between devices, body(): lax.psum(right_partial.astype(jnp.bfloat16), 'row').astype(jnp.float32)  92 us
    all_gather x1, waiting for transfers between devices, body(): grads_full = lax.all_gather(out_grads, 'row', axis=0, tiled=True)  91 us
    dot_general x3, matrix products, contract_rank(): lax.dot_general(first, second, (((1,), (1,)), ((), ())), preferred_elemen...  67.3 us
    dot_general x2, matrix products, contract_tokens(): lax.dot_general(first, second, (((0,), (0,)), ((), ())), preferred_elemen...  48.1 us
    psum x1, waiting for transfers between devices, body(): left_descent = lax.psum(left_partial, 'col')  41.2 us
    psum x1, blocking collectives, body(): lax.psum((jnp.sum(fisher * left_image * left_image), left_norm_term), ('r...  32.8 us
    convert_element_type x1, other arithmetic, body(): residual = (later_residual - right_step * right_image).astype(jnp.bfloat16)  32.5 us
    psum x1, blocking collectives, body(): lax.psum((jnp.sum(fisher * right_image * right_image), right_norm_term),...  32 us
  transfers between devices with their start and end apart: 4, of which 4 were waited for; matrix products, arithmetic and copies ran while one was open for 4% of the time, Pallas kernels for 0%

commit v1 on v0

--- a/solution.py
+++ b/solution.py
@@ -4,6 +4,12 @@
 from jax.sharding import PartitionSpec as P
 
 epsilon = 1e-06
+
+
+def add_all(block, mesh_axis):
+    pieces = lax.all_gather(block, mesh_axis, axis=0, tiled=False)
+    total = pieces.sum(axis=0)
+    return total
 
 
 def contract_rank(first, second):
@@ -41,7 +47,7 @@
     later_residual = early_residual - left_step * left_image
     weighted_later = (fisher * later_residual).astype(jnp.bfloat16)
     right_partial = contract_tokens(weighted_later, left_new)
-    right_descent = lax.psum(right_partial.astype(jnp.bfloat16), "row").astype(jnp.float32)
+    right_descent = add_all(right_partial.astype(jnp.bfloat16), "row").astype(jnp.float32)
     right_round = right_descent.astype(jnp.bfloat16)
     right_norm_term = jnp.sum(right_descent * right_descent) / row_count
     right_image = contract_rank(left_new, right_round)

time: 490 us -> 570 us (1.16)
  waiting for transfers between devices: 229 us -> 301 us
  other arithmetic: 42.5 us -> 51 us
    all_gather x0 -> x1, waiting for transfers between devices: none -> 164 us  [add_all(): pieces = lax.all_gather(block, mesh_axis, axis=0, tiled=False)]
    psum x1 -> x0, waiting for transfers between devices: 92 us -> none  [body(): lax.psum(right_partial.astype(jnp.bfloat16), 'row').astype(jnp.float32)]
    reduce_sum x0 -> x1, other arithmetic: none -> 7.13 us  [add_all(): total = pieces.sum(axis=0)]
  transfers between devices with their start and end apart: 4 -> 4, of which waited for: 4 -> 4; matrix products, arithmetic and copies ran while one was open for 4% -> 3% of each run, Pallas kernels for 0% -> 0%
where the time goes in v1:
time: 570 us
  waiting for transfers between devices  301 us (53%)
  matrix products  135 us (24%)
  blocking collectives  63.8 us (11%)
  other arithmetic  51 us (9%)
  between operations  17.6 us (3%)
    all_gather x1, waiting for transfers between devices, add_all(): pieces = lax.all_gather(block, mesh_axis, axis=0, tiled=False)  164 us
    all_gather x1, waiting for transfers between devices, body(): grads_full = lax.all_gather(out_grads, 'row', axis=0, tiled=True)  91 us
    dot_general x3, matrix products, contract_rank(): lax.dot_general(first, second, (((1,), (1,)), ((), ())), preferred_elemen...  67.4 us
    dot_general x2, matrix products, contract_tokens(): lax.dot_general(first, second, (((0,), (0,)), ((), ())), preferred_elemen...  48.2 us
    psum x1, waiting for transfers between devices, body(): left_descent = lax.psum(left_partial, 'col')  41.2 us
    psum x1, blocking collectives, body(): lax.psum((jnp.sum(fisher * left_image * left_image), left_norm_term), ('r...  32.8 us
    convert_element_type x1, other arithmetic, body(): residual = (later_residual - right_step * right_image).astype(jnp.bfloat16)  32.4 us
    psum x1, blocking collectives, body(): lax.psum((jnp.sum(fisher * right_image * right_image), right_norm_term),...  31 us
  transfers between devices with their start and end apart: 4, of which 4 were waited for; matrix products, arithmetic and copies ran while one was open for 3% of the time, Pallas kernels for 0%

profile of v1, /device:TPU:0, one launch (start us, length us, event | category | flops | bytes accessed | tf_op | source)
XLA Modules:
  0.0 569.6 jit_solution(9916728342933266504)
XLA Ops:
  7.2 0.0 all-gather.5.cloned.1.call-start
  7.2 0.7 all-gather.5.cloned.1.call-update
  7.9 0.0 all-gather.7.cloned.1.call-start
  7.9 0.7 all-gather.7.cloned.1.call-update
  8.6 0.0 all-reduce.4.cloned.1.call-start
  8.7 19.6 %convert_subtract_fusion = f32[1536,4608]{1,0:T(8,128)} fusion(bf16[1536,4608]{1,0:T(8,128)(2,1)} %param.7, bf16[1536,256]{1,0:T(8,128)(2,1)} %param.8, bf16[4608,256]{1,0:T(8,128)(2,1)} %param.9), kind=kOutput, calls=%fused_computation.2 | convolution fusion | flops 3638034432 | bytes 45613056 | tf_op jit(solution)/shard_map/dot_general | solution.py:16
  28.3 0.0 copy-start
  28.3 3.6 all-gather.5.cloned.1.call-done
  31.9 91.0 %all-gather.7.cloned.1.call-done = bf16[512,4608]{1,0:T(8,128)(2,1)} async-done(((bf16[128,4608]{1,0:T(8,128)(2,1)}), bf16[512,4608]{1,0:T(8,128)(2,1)}) %all-gather.7.cloned.1.call-update) | async-done | bytes 4718608 | tf_op jit(solution)/shard_map/all_gather | solution.py:31
  122.9 17.9 %fusion.1 = f32[1536,4608]{1,0:T(8,128)} fusion(bf16[1536,4608]{1,0:T(8,128)(2,1)} %param.7, bf16[512,1536]{1,0:T(8,128)(2,1)} %all-gather.5.cloned.1.call-done, bf16[512,4608]{1,0:T(8,128)(2,1)} %all-gather.7.cloned.1.call-done), kind=kOutput, calls=%fused_computation.5 | convolution fusion | flops 7276068864 | bytes 48758784 | tf_op jit(solution)/shard_map/dot_general | solution.py:22
  140.8 0.0 copy-done
  140.8 19.9 %fusion.4 = f32[1536,256]{1,0:T(8,128)} fusion(bf16[4608,256]{1,0:T(8,128)(2,1)S(1)} %copy-done, f32[1536,4608]{1,0:T(8,128)} %fusion.1, f32[1536,4608]{1,0:T(8,128)} %convert_subtract_fusion), kind=kOutput, calls=%fused_computation.12 | convolution fusion | flops 3638034432 | bytes 60555264 | tf_op jit(solution)/shard_map/dot_general | solution.py:37
  160.7 0.0 all-reduce.4.cloned.1.call-update
  160.8 0.2 all-gather.9.cloned.1.call-start
  161.0 41.2 %all-reduce.4.cloned.1.call-done = f32[1536,256]{1,0:T(8,128)} async-done(((f32[1536,256]{1,0:T(8,128)}), f32[1536,256]{1,0:T(8,128)}) %all-reduce.4.cloned.1.call-update) | async-done | bytes 1572880 | tf_op jit(solution)/shard_map/psum | solution.py:38
  202.2 2.4 multiply_reduce_fusion
  205.2 23.7 %fusion.2 = (f32[]{:T(128)}, f32[1536,4608]{1,0:T(8,128)}) fusion(f32[1536,4608]{1,0:T(8,128)} %fusion.1, bf16[4608,256]{1,0:T(8,128)(2,1)S(1)} %copy-done, f32[1536,256]{1,0:T(8,128)} %all-reduce.4.cloned.1.call-done), kind=kOutput, calls=%fused_computation.6 | convolution fusion | flops 3645505536 | bytes 60555268 | tf_op jit(solution)/shard_map/dot_general | solution.py:16
  228.9 32.8 %all-reduce.1 = (f32[]{:T(128)}, f32[]{:T(128)}) all-reduce(f32[]{:T(128)S(6)} %div.12, f32[]{:T(128)} %get-tuple-element.7), channel_id=1, replica_groups=mesh['grp'=2,'row'=4,'col'=4] {'row','col'}, use_global_device_ids=true, to_apply=%region_2.0 | all-reduce | flops 2 | bytes 16 | tf_op jit(solution)/shard_map/psum | solution.py:42
  263.1 1.8 add_convert_fusion
  264.8 0.0 copy-start.1
  264.9 30.2 %fusion.6 = bf16[4608,256]{1,0:T(8,128)(2,1)} fusion(bf16[1536,256]{1,0:T(8,128)(2,1)S(1)} %add_convert_fusion, f32[1536,4608]{1,0:T(8,128)} %fusion.1, f32[1536,4608]{1,0:T(8,128)} %convert_subtract_fusion, f32[1536,4608]{1,0:T(8,128)} %get-tuple-element.8, f32[]{:T(128)S(6)} %div.13), kind=kOutput, calls=%fused_computation.14 | convolution fusion | flops 3653369856 | bytes 88080384 | tf_op jit(solution)/shard_map/dot_general | solution.py:22
  295.1 0.0 all-gather.9.cloned.1.call-update
  295.1 164.1 %all-gather.9.cloned.1.call-done = bf16[18432,256]{1,0:T(8,128)(2,1)} async-done(((bf16[4608,256]{1,0:T(8,128)(2,1)}), bf16[18432,256]{1,0:T(8,128)(2,1)}) %all-gather.9.cloned.1.call-update) | async-done | bytes 9437200 | tf_op jit(solution)/shard_map/all_gather | solution.py:10
  459.3 7.1 %reduce_sum.50 = bf16[4608,256]{1,0:T(8,128)(2,1)} reduce(bf16[4,4608,256]{2,1,0:T(8,128)(2,1)} %bitcast.10, bf16[]{:T(256)} %constant.11.clone.1), dimensions={0}, to_apply=%region_5.0 | reduce | flops 3538944 | bytes 11796482 | tf_op jit(solution)/shard_map/reduce_sum | solution.py:11
  466.4 3.5 fusion.7
  469.9 0.0 copy-done.1
  469.9 24.1 %fusion.3 = (f32[]{:T(128)}, f32[1536,4608]{1,0:T(8,128)}) fusion(f32[1536,4608]{1,0:T(8,128)} %fusion.1, bf16[1536,256]{1,0:T(8,128)(2,1)S(1)} %add_convert_fusion, bf16[4608,256]{1,0:T(8,128)(2,1)} %reduce_sum.50), kind=kOutput, calls=%fused_computation.7 | convolution fusion | flops 3645112320 | bytes 59768836 | tf_op jit(solution)/shard_map/dot_general | solution.py:16
  494.6 31.0 %all-reduce = (f32[]{:T(128)}, f32[]{:T(128)}) all-reduce(f32[]{:T(128)S(6)} %div.14, f32[]{:T(128)} %get-tuple-element.9), channel_id=1, replica_groups=mesh['grp'=2,'row'=4,'col'=4] {'row','col'}, use_global_device_ids=true, to_apply=%region_7.0 | all-reduce | flops 2 | bytes 16 | tf_op jit(solution)/shard_map/psum | solution.py:54
  526.9 3.8 fusion.9
  530.7 32.4 %subtract_convert_fusion = bf16[1536,4608]{1,0:T(8,128)(2,1)} fusion(f32[1536,4608]{1,0:T(8,128)} %get-tuple-element.10, f32[]{:T(128)S(6)} %div.15, f32[1536,4608]{1,0:T(8,128)} %convert_subtract_fusion, f32[1536,4608]{1,0:T(8,128)} %get-tuple-element.8, f32[]{:T(128)S(6)} %div.13), kind=kLoop, calls=%fused_computation.8 | loop fusion | flops 35389440 | bytes 99090440 | tf_op jit(solution)/shard_map/convert_element_type | solution.py:59
Async XLA Ops:
  7.2 24.8 %all-gather.5.cloned.1.call-start = ((), (), s32[]{:S(2)}) async-start(), calls=%async_computation | async-start | bytes 1966080 | tf_op jit(solution)/shard_map/all_gather | solution.py:30
  7.9 115.0 %all-gather.7.cloned.1.call-start = ((), (), s32[]{:S(2)}) async-start(), calls=%async_computation.1 | async-start | bytes 5898240 | tf_op jit(solution)/shard_map/all_gather | solution.py:31
  8.6 193.5 %all-reduce.4.cloned.1.call-start = ((), (), s32[]{:S(2)}) async-start(), calls=%async_computation.2 | async-start | bytes 3145728 | tf_op jit(solution)/shard_map/psum | solution.py:38
  28.3 112.5 %copy-start = (bf16[4608,256]{1,0:T(8,128)(2,1)S(1)}, bf16[4608,256]{1,0:T(8,128)(2,1)}, u32[]{:S(2)}) copy-start(bf16[4608,256]{1,0:T(8,128)(2,1)} %param.9) | copy-start | bytes 7077892
  160.8 298.5 %all-gather.9.cloned.1.call-start = ((), (), s32[]{:S(2)}) async-start(), calls=%async_computation.3 | async-start | bytes 11796480 | tf_op jit(solution)/shard_map/all_gather | solution.py:10
  264.8 205.0 %copy-start.1 = (bf16[1536,256]{1,0:T(8,128)(2,1)}, bf16[1536,256]{1,0:T(8,128)(2,1)S(1)}, u32[]{:S(2)}) copy-start(bf16[1536,256]{1,0:T(8,128)(2,1)S(1)} %add_convert_fusion) | copy-start | bytes 2359300
Sparse Core Ops, SparseCore 0:
  9.5 22.3 all-gather.4
  33.5 89.3 all-gather.6
  160.9 41.2 all-reduce.3
  295.2 163.9 all-gather.8
